TPU v7x, 512 devices: a whole 4x4x16 slice. The times are simulated.
512 devices in a mesh: tile: 128 (over z, x, core), lev: 4 (over y).
Axes of the slice: x: 4, y: 4, z: 16, core: 2. Of those that a mesh axis runs over, the one named last changes fastest.
Arguments:
- probes: bfloat16 [512, 32, 8, 128], P('tile', None, 'lev'), may hold values from -1 to 1, as said below
- stddev: float32 [512, 32, 128], P('tile'), may hold values from 0.5 to 2
- diffusivity: float32 [128], replicated, may hold values from 0.03 to 0.24
- counts: int32 [128, 128], P('tile'), may hold values from 0 to 16, as said below
- columns: int32 [128, 128, 16], P('tile'), may hold values from 0 to 127
- jacobian: bfloat16 [128, 256, 32], P('tile'), may hold values from -1 to 1
- offsets: int32 [128, 256], replicated, may hold values from 0 to 96
- obs_weights: float32 [128, 256], replicated, may hold values from 0.25 to 4
Outputs:
- hessian_probe: float32 [512, 32, 8, 128], P('tile', None, 'lev')
- trace_share: float32 [128], P('tile')
Inputs may be any that keep to these rules, and one draw needn't show every extreme that they name: `counts`: in every draw one section receives 16 observations from every tile. `columns`: slots at or past counts[t,d] are unused. `probes`: each entry is +1 or -1.
All inputs are finite; a program needn't handle non-finite values.
Results may differ from a plain program's by a relative error of at most 0.00045.
The roundings to bfloat16 on the way count: a program that leaves them out, or rounds other values in their place, can miss the bound.
Values may be sent and summed in bfloat16 or wider, within the bound.
No kernel may reach another device: no remote copies, remote signals or barrier semaphores. Data moves between devices by JAX's collectives and lax.ppermute only.
A program may use at most 64 MiB of HBM per device.

v0:
```python
import math
import jax
import jax.numpy as jnp
from jax import lax
from jax.sharding import PartitionSpec as P

LEV = 128
CH = 256
PROBES = 8
NSTEP = 2


def padded_2(cells, sides, width):
    for axis, dim in sides:
        count = lax.axis_size(axis)
        head = lax.slice_in_dim(cells, 0, width, axis=dim)
        tail = lax.slice_in_dim(cells, cells.shape[dim] - width, cells.shape[dim], axis=dim)
        cells = jnp.concatenate(
            [
                lax.ppermute(tail, axis, [(i, (i + 1) % count) for i in range(count)]),
                cells,
                lax.ppermute(head, axis, [((i + 1) % count, i) for i in range(count)]),
            ],
            axis=dim,
        )
    return cells


def diffuse(extended, diffusivity):
    middle = extended[1:-1]
    padded = jnp.pad(middle, ((0, 0), (1, 1), (0, 0), (0, 0)))
    laplace = extended[2:] + extended[:-2] + padded[:, 2:] + padded[:, :-2] - 4.0 * middle
    return middle + diffusivity * laplace


def smooth(profile, diffusivity):
    for repeat in range(NSTEP):
        extended = padded_2(profile, (("tile", 0),), 1)
        profile = diffuse(extended, diffusivity)
    return profile


def band_matrix(jacobian_rows, offset_rows):
    band_width = jacobian_rows.shape[-1]
    pad_spec = [(0, 0)] * (jacobian_rows.ndim - 1) + [(0, LEV - band_width)]
    widened = jnp.pad(jacobian_rows, pad_spec)
    bit_count = max((LEV - 1).bit_length(), 1)
    for bit_number in range(bit_count):
        step_size = 1 << bit_number
        moved = jnp.roll(widened, step_size, axis=-1)
        chosen = (offset_rows // step_size % 2 == 1)[..., None]
        widened = jnp.where(chosen, moved, widened)
    return widened


def respond(rows_in, dense_map, weights):
    brightness = lax.dot_general(
        rows_in, dense_map, (((1,), (1,)), ((), ())), preferred_element_type=jnp.float32
    )
    weighted = weights * brightness
    energy = jnp.sum(brightness * weighted, axis=1)
    adjoint = jnp.dot(weighted.astype(jnp.bfloat16), dense_map, preferred_element_type=jnp.float32)
    return (adjoint.astype(jnp.bfloat16), energy)


def body(probes, stddev, diffusivity, counts, columns, jacobian, offsets, obs_weights):
    tile_count = lax.axis_size("tile")
    my_section = lax.axis_index("tile")
    row_count, col_count, probe_count, levels = probes.shape
    slot_count = columns.shape[2]
    cell_count = row_count * col_count
    spread = stddev[:, :, None, :]
    profile = (spread * smooth(probes.astype(jnp.float32), diffusivity)).astype(jnp.bfloat16)
    flat_profile = profile.reshape(cell_count, probe_count, levels)
    targets = columns[0]
    live_slots = jnp.arange(slot_count, dtype=jnp.int32)[None, :] < counts[0][:, None]
    cell_ids = jnp.arange(cell_count, dtype=jnp.int32)
    selector = ((targets[:, :, None] == cell_ids[None, None, :]) & live_slots[:, :, None]).astype(
        jnp.bfloat16
    )
    outgoing = jnp.einsum(
        "tkn,npl->tkpl", selector, flat_profile, preferred_element_type=jnp.float32
    ).astype(jnp.bfloat16)
    own_offsets = lax.dynamic_index_in_dim(offsets, my_section, 0, keepdims=False)
    dense_map = band_matrix(jacobian[0], own_offsets)
    weights = lax.dynamic_index_in_dim(obs_weights, my_section, 0, keepdims=False)
    arrived = lax.all_to_all(outgoing, "tile", split_axis=0, concat_axis=0, tiled=True)
    sources, slot_here, probe_here, level_here = arrived.shape
    group_size = math.gcd(sources, 8)
    stacked = arrived.reshape(
        sources // group_size, group_size * slot_here * probe_here, level_here
    )

    def radiate(batch_rows):
        return respond(batch_rows, dense_map, weights)

    adjoint, energy = lax.map(radiate, stacked)
    energy = energy.reshape(sources, slot_here, probe_here).sum(axis=2)
    adjoints_here = adjoint.reshape(arrived.shape)
    returned = lax.all_to_all(adjoints_here, "tile", split_axis=0, concat_axis=0, tiled=True)
    section_part = jnp.sum(energy).reshape(1)
    totals = lax.psum(section_part, "lev")
    trace_share = totals * (1.0 / (PROBES * tile_count * slot_count * CH))
    gradient = jnp.einsum("tkn,tkpl->npl", selector, returned, preferred_element_type=jnp.float32)
    gradient = gradient.reshape(row_count, col_count, probe_count, levels)
    hessian = smooth(spread * gradient, diffusivity)
    return (hessian, trace_share)


def solution(mesh):
    placed = (
        P("tile", None, "lev", None),
        P("tile", None, None),
        P(),
        P("tile", None),
        P("tile", None, None),
        P("tile", None, None),
        P(),
        P(),
    )
    return jax.shard_map(
        body,
        mesh=mesh,
        in_specs=placed,
        out_specs=(P("tile", None, "lev", None), P("tile")),
        check_vma=False,
    )
```

profile of v0, /device:TPU:32, one launch (start us, length us, event | category | flops | bytes accessed | tf_op | source)
XLA Modules:
  0.0 203.5 jit_solution(3389362068707142357)
XLA Ops:
  0.7 0.8 fusion.54
  1.5 3.7 %collective-permute-start = (f32[1,32,2,128]{3,2,1,0:T(2,128)S(1)}, f32[1,32,2,128]{3,2,1,0:T(2,128)S(1)}, u32[]{:S(2)}, u32[]{:S(2)}) collective-permute-start(f32[1,32,2,128]{3,2,1,0:T(2,128)S(1)} %get-tuple-element.61), channel_id=1, source_target_pairs={{4,0},{8,4},{12,8},{16,12},{20,16},{24,20},{28,24},{32,28},{36,32}... | collective-permute-start | bytes 98312 | tf_op jit(solution)/shard_map/ppermute | solution.py:22
  5.1 1.9 collective-permute-start.1
  7.0 0.9 convert_element_type.23
  7.9 4.5 %collective-permute-done.1 = f32[1,32,2,128]{3,2,1,0:T(2,128)S(1)} collective-permute-done((f32[1,32,2,128]{3,2,1,0:T(2,128)S(1)}, f32[1,32,2,128]{3,2,1,0:T(2,128)S(1)}, u32[]{:S(2)}, u32[]{:S(2)}) %collective-permute-start.1) | collective-permute-done | bytes 32800 | tf_op jit(solution)/shard_map/ppermute | solution.py:20
  12.5 0.8 multiply_add_fusion.2
  13.3 1.9 collective-permute-start.2
  15.2 2.4 %collective-permute-start.3 = (f32[1,32,2,128]{3,2,1,0:T(2,128)S(1)}, f32[1,32,2,128]{3,2,1,0:T(2,128)S(1)}, u32[]{:S(2)}, u32[]{:S(2)}) collective-permute-start(f32[1,32,2,128]{3,2,1,0:T(2,128)S(1)} %get-tuple-element.58), channel_id=1, source_target_pairs={{0,4},{4,8},{8,12},{12,16},{16,20},{20,24},{24,28},{28,32},{32,36}... | collective-permute-start | bytes 98312 | tf_op jit(solution)/shard_map/ppermute | solution.py:20
  17.6 0.7 iota_compare_fusion.1
  18.3 4.3 %collective-permute-done.3 = f32[1,32,2,128]{3,2,1,0:T(2,128)S(1)} collective-permute-done((f32[1,32,2,128]{3,2,1,0:T(2,128)S(1)}, f32[1,32,2,128]{3,2,1,0:T(2,128)S(1)}, u32[]{:S(2)}, u32[]{:S(2)}) %collective-permute-start.3) | collective-permute-done | bytes 32800 | tf_op jit(solution)/shard_map/ppermute | solution.py:20
  22.6 1.0 multiply_convert_fusion.2
  23.6 0.5 convolution_convert_fusion.1
  24.1 2.1 %copy.22 = bf16[128,16,2,128]{3,2,1,0:T(2,128)(2,1)} copy(bf16[128,16,2,128]{3,0,2,1:T(8,128)(2,1)S(1)} %convolution_convert_fusion.1) | data formatting | bytes 2097152 | tf_op jit(solution)/shard_map/convert_element_type | solution.py:83
  26.2 19.1 %all-to-all-start = ((bf16[128,16,2,128]{3,2,1,0:T(2,128)(2,1)}), bf16[128,16,2,128]{3,2,1,0:T(2,128)(2,1)S(1)}, u32[]{:S(2)}, u32[]{:S(2)}) async-start(bf16[128,16,2,128]{3,2,1,0:T(2,128)(2,1)} %copy.22), calls=%async_computation | async-start | bytes 2097152 | tf_op jit(solution)/shard_map/all_to_all | solution.py:87
  46.0 0.1 maximum_select_fusion.1
  46.2 0.1 maximum_select_fusion.2
  46.6 0.7 constant_dynamic-slice_fusion.1
  47.7 53.0 %all-to-all-done = bf16[128,16,2,128]{3,2,1,0:T(2,128)(2,1)S(1)} async-done(((bf16[128,16,2,128]{3,2,1,0:T(2,128)(2,1)}), bf16[128,16,2,128]{3,2,1,0:T(2,128)(2,1)S(1)}, u32[]{:S(2)}, u32[]{:S(2)}) %all-to-all-start) | async-done | bytes 1048608 | tf_op jit(solution)/shard_map/all_to_all | solution.py:87
  100.7 9.9 %while.12 = (s32[]{:T(128)}, bf16[16,256,128]{2,1,0:T(8,128)(2,1)S(1)}, f32[16,256]{1,0:T(8,128)S(1)}, f32[256]{0:T(256)S(1)}, bf16[16,256,128]{2,1,0:T(8,128)(2...) while((s32[]{:T(128)}, bf16[16,256,128]{2,1,0:T(8,128)(2,1)S(1)}, f32[16,256]{1,0:T(8,128)S(1)}, ...), condition=%wide.region_2.3_spmd, body=%wide.region_0.2_spmd.sunk | while | flops 33914624 | bytes 791657 | solution.py:97
  100.7 0.2 fusion.63
  101.0 0.3 fusion.64
  101.3 0.2 fusion.63
  101.6 0.3 fusion.64
  102.0 0.2 fusion.63
  102.2 0.3 fusion.64
  102.6 0.2 fusion.63
  102.9 0.3 fusion.64
  103.2 0.2 fusion.63
  103.5 0.3 fusion.64
  103.8 0.2 fusion.63
  104.1 0.3 fusion.64
  104.4 0.2 fusion.63
  104.7 0.3 fusion.64
  105.1 0.2 fusion.63
  105.4 0.3 fusion.64
  105.7 0.2 fusion.63
  106.0 0.3 fusion.64
  106.3 0.2 fusion.63
  106.6 0.3 fusion.64
  106.9 0.2 fusion.63
  107.2 0.3 fusion.64
  107.6 0.2 fusion.63
  107.8 0.3 fusion.64
  108.2 0.2 fusion.63
  108.5 0.3 fusion.64
  108.8 0.2 fusion.63
  109.1 0.3 fusion.64
  109.4 0.2 fusion.63
  109.7 0.3 fusion.64
  110.1 0.2 fusion.63
  110.3 0.3 fusion.64
  110.7 0.2 copy.24
  110.9 61.9 %all_to_all.10 = bf16[128,16,2,128]{3,1,2,0:T(8,128)(2,1)S(1)} all-to-all(bf16[128,16,2,128]{3,1,2,0:T(8,128)(2,1)S(1)} %copy.24), channel_id=1, replica_groups=mesh['tile'=128,'lev'=4] {'tile'}, dimensions={0} | all-to-all | bytes 2097152 | tf_op jit(solution)/shard_map/all_to_all | solution.py:100
  172.7 0.8 fusion.8
  173.6 0.1 copy_multiply_fusion
  173.7 3.4 %collective-permute-start.4 = (f32[1,32,2,128]{3,2,1,0:T(2,128)S(1)}, f32[1,32,2,128]{3,2,1,0:T(2,128)S(1)}, u32[]{:S(2)}, u32[]{:S(2)}) collective-permute-start(f32[1,32,2,128]{3,2,1,0:T(2,128)S(1)} %get-tuple-element.55), channel_id=1, source_target_pairs={{4,0},{8,4},{12,8},{16,12},{20,16},{24,20},{28,24},{32,28},{36,32}... | collective-permute-start | bytes 98312 | tf_op jit(solution)/shard_map/ppermute | solution.py:22
  177.1 1.9 collective-permute-start.5
  179.1 5.4 %collective-permute-done.5 = f32[1,32,2,128]{3,2,1,0:T(2,128)S(1)} collective-permute-done((f32[1,32,2,128]{3,2,1,0:T(2,128)S(1)}, f32[1,32,2,128]{3,2,1,0:T(2,128)S(1)}, u32[]{:S(2)}, u32[]{:S(2)}) %collective-permute-start.5) | collective-permute-done | bytes 32800 | tf_op jit(solution)/shard_map/ppermute | solution.py:20
  184.5 0.1 multiply_add_fusion.1
  184.6 1.9 collective-permute-start.6
  186.6 2.4 %collective-permute-start.7 = (f32[1,32,2,128]{3,2,1,0:T(2,128)S(1)}, f32[1,32,2,128]{3,2,1,0:T(2,128)S(1)}, u32[]{:S(2)}, u32[]{:S(2)}) collective-permute-start(f32[1,32,2,128]{3,2,1,0:T(2,128)S(1)} %get-tuple-element.54), channel_id=1, source_target_pairs={{0,4},{4,8},{8,12},{12,16},{16,20},{20,24},{24,28},{28,32},{32,36}... | collective-permute-start | bytes 98312 | tf_op jit(solution)/shard_map/ppermute | solution.py:20
  189.0 0.6 reduce_sum.17
  189.6 11.3 %psum.7 = f32[1]{0:T(128)} all-reduce(f32[1]{0:T(128)} %bitcast.17), channel_id=1, replica_groups=mesh['tile'=128,'lev'=4] {'lev'}, use_global_device_ids=true, to_apply=%region_4.5 | all-reduce | flops 1 | bytes 8 | tf_op jit(solution)/shard_map/psum | solution.py:102
  201.6 0.8 multiply_add_fusion
  (52 shorter events, 2.1 us)
Async XLA Ops:
  0.6 44.8 %copy-start = (s32[128,256]{1,0:T(8,128)S(1)}, s32[128,256]{1,0:T(8,128)}, u32[]{:S(2)}) copy-start(s32[128,256]{1,0:T(8,128)} %param.16) | copy-start | bytes 393220
  0.6 23.0 %copy-start.3 = (s32[1,128,16]{1,2,0:T(8,128)S(1)}, s32[1,128,16]{1,2,0:T(8,128)}, u32[]{:S(2)}) copy-start(s32[1,128,16]{1,2,0:T(8,128)} %param.14) | copy-start | bytes 24580
  1.5 6.5 %collective-permute-start = (f32[1,32,2,128]{3,2,1,0:T(2,128)S(1)}, f32[1,32,2,128]{3,2,1,0:T(2,128)S(1)}, u32[]{:S(2)}, u32[]{:S(2)}) collective-permute-start(f32[1,32,2,128]{3,2,1,0:T(2,128)S(1)} %get-tuple-element.61), channel_id=1, source_target_pairs={{4,0},{8,4},{12,8},{16,12},{20,16},{24,20},{28,24},{32,28},{36,32}... | collective-permute-start | bytes 98312 | tf_op jit(solution)/shard_map/ppermute | solution.py:22
  5.1 7.3 %collective-permute-start.1 = (f32[1,32,2,128]{3,2,1,0:T(2,128)S(1)}, f32[1,32,2,128]{3,2,1,0:T(2,128)S(1)}, u32[]{:S(2)}, u32[]{:S(2)}) collective-permute-start(f32[1,32,2,128]{3,2,1,0:T(2,128)S(1)} %get-tuple-element.62), channel_id=1, source_target_pairs={{0,4},{4,8},{8,12},{12,16},{16,20},{20,24},{24,28},{28,32},{32,36}... | collective-permute-start | bytes 98312 | tf_op jit(solution)/shard_map/ppermute | solution.py:20
  13.3 5.0 %collective-permute-start.2 = (f32[1,32,2,128]{3,2,1,0:T(2,128)S(1)}, f32[1,32,2,128]{3,2,1,0:T(2,128)S(1)}, u32[]{:S(2)}, u32[]{:S(2)}) collective-permute-start(f32[1,32,2,128]{3,2,1,0:T(2,128)S(1)} %get-tuple-element.57), channel_id=1, source_target_pairs={{4,0},{8,4},{12,8},{16,12},{20,16},{24,20},{28,24},{32,28},{36,32}... | collective-permute-start | bytes 98312 | tf_op jit(solution)/shard_map/ppermute | solution.py:22
  15.2 7.3 %collective-permute-start.3 = (f32[1,32,2,128]{3,2,1,0:T(2,128)S(1)}, f32[1,32,2,128]{3,2,1,0:T(2,128)S(1)}, u32[]{:S(2)}, u32[]{:S(2)}) collective-permute-start(f32[1,32,2,128]{3,2,1,0:T(2,128)S(1)} %get-tuple-element.58), channel_id=1, source_target_pairs={{0,4},{4,8},{8,12},{12,16},{16,20},{20,24},{24,28},{28,32},{32,36}... | collective-permute-start | bytes 98312 | tf_op jit(solution)/shard_map/ppermute | solution.py:20
  26.2 19.1 %copy-start.2 = (bf16[1,256,32]{1,2,0:T(8,128)(2,1)S(1)}, bf16[1,256,32]{1,2,0:T(8,128)(2,1)}, u32[]{:S(2)}) copy-start(bf16[1,256,32]{1,2,0:T(8,128)(2,1)} %param.15) | copy-start | bytes 49156
  26.2 74.6 %all-to-all-start = ((bf16[128,16,2,128]{3,2,1,0:T(2,128)(2,1)}), bf16[128,16,2,128]{3,2,1,0:T(2,128)(2,1)S(1)}, u32[]{:S(2)}, u32[]{:S(2)}) async-start(bf16[128,16,2,128]{3,2,1,0:T(2,128)(2,1)} %copy.22), calls=%async_computation | async-start | bytes 2097152 | tf_op jit(solution)/shard_map/all_to_all | solution.py:87
  172.7 0.8 copy-start.1
  172.7 11.7 %copy-start.4 = (f32[128]{0:T(128)S(1)}, f32[128]{0:T(128)}, u32[]{:S(2)}) copy-start(f32[128]{0:T(128)} %param.12) | copy-start | bytes 1540
  173.7 5.3 %collective-permute-start.4 = (f32[1,32,2,128]{3,2,1,0:T(2,128)S(1)}, f32[1,32,2,128]{3,2,1,0:T(2,128)S(1)}, u32[]{:S(2)}, u32[]{:S(2)}) collective-permute-start(f32[1,32,2,128]{3,2,1,0:T(2,128)S(1)} %get-tuple-element.55), channel_id=1, source_target_pairs={{4,0},{8,4},{12,8},{16,12},{20,16},{24,20},{28,24},{32,28},{36,32}... | collective-permute-start | bytes 98312 | tf_op jit(solution)/shard_map/ppermute | solution.py:22
  177.1 7.3 %collective-permute-start.5 = (f32[1,32,2,128]{3,2,1,0:T(2,128)S(1)}, f32[1,32,2,128]{3,2,1,0:T(2,128)S(1)}, u32[]{:S(2)}, u32[]{:S(2)}) collective-permute-start(f32[1,32,2,128]{3,2,1,0:T(2,128)S(1)} %get-tuple-element.56), channel_id=1, source_target_pairs={{0,4},{4,8},{8,12},{12,16},{16,20},{20,24},{24,28},{28,32},{32,36}... | collective-permute-start | bytes 98312 | tf_op jit(solution)/shard_map/ppermute | solution.py:20
  184.6 17.0 %collective-permute-start.6 = (f32[1,32,2,128]{3,2,1,0:T(2,128)S(1)}, f32[1,32,2,128]{3,2,1,0:T(2,128)S(1)}, u32[]{:S(2)}, u32[]{:S(2)}) collective-permute-start(f32[1,32,2,128]{3,2,1,0:T(2,128)S(1)} %get-tuple-element.53), channel_id=1, source_target_pairs={{4,0},{8,4},{12,8},{16,12},{20,16},{24,20},{28,24},{32,28},{36,32}... | collective-permute-start | bytes 98312 | tf_op jit(solution)/shard_map/ppermute | solution.py:22
  186.6 15.0 %collective-permute-start.7 = (f32[1,32,2,128]{3,2,1,0:T(2,128)S(1)}, f32[1,32,2,128]{3,2,1,0:T(2,128)S(1)}, u32[]{:S(2)}, u32[]{:S(2)}) collective-permute-start(f32[1,32,2,128]{3,2,1,0:T(2,128)S(1)} %get-tuple-element.54), channel_id=1, source_target_pairs={{0,4},{4,8},{8,12},{12,16},{16,20},{20,24},{24,28},{28,32},{32,36}... | collective-permute-start | bytes 98312 | tf_op jit(solution)/shard_map/ppermute | solution.py:20
where the time goes:
time: 204 us
  blocking collectives  73.2 us (36%)
  waiting for transfers between devices  67.2 us (33%)
  starting transfers between devices  38.6 us (19%)
  matrix products  10.1 us (5%)
  other arithmetic  5.97 us (3%)
  local copies, waits for them, and re-layouts  5.19 us (3%)
  between operations  2.76 us (1%)
    all_to_all x1, blocking collectives, body(): lax.all_to_all(adjoints_here, 'tile', split_axis=0, concat_axis=0, tiled=...  61.9 us
    all_to_all x1, waiting for transfers between devices, body(): lax.all_to_all(outgoing, 'tile', split_axis=0, concat_axis=0, tiled=True)  53 us
    all_to_all x1, starting transfers between devices, body(): lax.all_to_all(outgoing, 'tile', split_axis=0, concat_axis=0, tiled=True)  19.1 us
    ppermute x4, waiting for transfers between devices, padded_2(): lax.ppermute(tail, axis, [(i, (i + 1) % count) for i in range(count)])  14.2 us
    psum x1, blocking collectives, body(): totals = lax.psum(section_part, 'lev')  11.3 us
    ppermute x4, starting transfers between devices, padded_2(): lax.ppermute(head, axis, [((i + 1) % count, i) for i in range(count)])  10.9 us
    ppermute x4, starting transfers between devices, padded_2(): lax.ppermute(tail, axis, [(i, (i + 1) % count) for i in range(count)])  8.65 us
    dot_general x16, matrix products, respond(): jnp.dot(weighted.astype(jnp.bfloat16), dense_map, preferred_element_type=...  5.18 us
  transfers between devices with their start and end apart: 9, of which 4 were waited for; matrix products, arithmetic and copies ran while one was open for 2% of the time, Pallas kernels for 0%

commit v1 on v0

--- a/solution.py
+++ b/solution.py
@@ -99,7 +99,9 @@
     adjoints_here = adjoint.reshape(arrived.shape)
     returned = lax.all_to_all(adjoints_here, "tile", split_axis=0, concat_axis=0, tiled=True)
     section_part = jnp.sum(energy).reshape(1)
-    totals = lax.psum(section_part, "lev")
+    totals = section_part
+    for hop in (1, 2):
+        totals = totals + lax.ppermute(totals, "lev", [(dev, dev ^ hop) for dev in range(4)])
     trace_share = totals * (1.0 / (PROBES * tile_count * slot_count * CH))
     gradient = jnp.einsum("tkn,tkpl->npl", selector, returned, preferred_element_type=jnp.float32)
     gradient = gradient.reshape(row_count, col_count, probe_count, levels)

time: 204 us -> 207 us (1.015)
  the two profiles are of different devices: /device:TPU:32 before, /device:TPU:56 now
where the time goes in v1:
time: 207 us; the launch traced here: 206 us
  waiting for transfers between devices  72.9 us (35%)
  blocking collectives  61.9 us (30%)
  starting transfers between devices  45.7 us (22%)
  matrix products  10.1 us (5%)
  other arithmetic  5.97 us (3%)
  local copies, waits for them, and re-layouts  5.2 us (3%)
  between operations  3.89 us (2%)
    all_to_all x1, blocking collectives, body(): lax.all_to_all(adjoints_here, 'tile', split_axis=0, concat_axis=0, tiled=...  61.9 us
    all_to_all x1, waiting for transfers between devices, body(): lax.all_to_all(outgoing, 'tile', split_axis=0, concat_axis=0, tiled=True)  53 us
    all_to_all x1, starting transfers between devices, body(): lax.all_to_all(outgoing, 'tile', split_axis=0, concat_axis=0, tiled=True)  19.1 us
    ppermute x4, waiting for transfers between devices, padded_2(): lax.ppermute(tail, axis, [(i, (i + 1) % count) for i in range(count)])  14.2 us
    ppermute x4, starting transfers between devices, padded_2(): lax.ppermute(head, axis, [((i + 1) % count, i) for i in range(count)])  10.9 us
    ppermute x4, starting transfers between devices, padded_2(): lax.ppermute(tail, axis, [(i, (i + 1) % count) for i in range(count)])  8.65 us
    ppermute x2, starting transfers between devices, body(): lax.ppermute(totals, 'lev', [(dev, dev ^ hop) for dev in range(4)])  7.06 us
    ppermute x2, waiting for transfers between devices, body(): lax.ppermute(totals, 'lev', [(dev, dev ^ hop) for dev in range(4)])  5.64 us
  transfers between devices with their start and end apart: 11, of which 6 were waited for; matrix products, arithmetic and copies ran while one was open for 2% of the time, Pallas kernels for 0%

profile of v1, /device:TPU:56, one launch (start us, length us, event | category | flops | bytes accessed | tf_op | source)
XLA Modules:
  0.0 206.0 jit_solution(5120154758857040624)
XLA Ops:
  0.7 0.8 fusion.54
  1.5 3.7 %collective-permute-start = (f32[1,32,2,128]{3,2,1,0:T(2,128)S(1)}, f32[1,32,2,128]{3,2,1,0:T(2,128)S(1)}, u32[]{:S(2)}, u32[]{:S(2)}) collective-permute-start(f32[1,32,2,128]{3,2,1,0:T(2,128)S(1)} %get-tuple-element.61), channel_id=1, source_target_pairs={{4,0},{8,4},{12,8},{16,12},{20,16},{24,20},{28,24},{32,28},{36,32}... | collective-permute-start | bytes 98312 | tf_op jit(solution)/shard_map/ppermute | solution.py:22
  5.1 1.9 collective-permute-start.1
  7.0 0.9 convert_element_type.23
  7.9 4.5 %collective-permute-done.1 = f32[1,32,2,128]{3,2,1,0:T(2,128)S(1)} collective-permute-done((f32[1,32,2,128]{3,2,1,0:T(2,128)S(1)}, f32[1,32,2,128]{3,2,1,0:T(2,128)S(1)}, u32[]{:S(2)}, u32[]{:S(2)}) %collective-permute-start.1) | collective-permute-done | bytes 32800 | tf_op jit(solution)/shard_map/ppermute | solution.py:20
  12.5 0.8 multiply_add_fusion.2
  13.3 1.9 collective-permute-start.2
  15.2 2.4 %collective-permute-start.3 = (f32[1,32,2,128]{3,2,1,0:T(2,128)S(1)}, f32[1,32,2,128]{3,2,1,0:T(2,128)S(1)}, u32[]{:S(2)}, u32[]{:S(2)}) collective-permute-start(f32[1,32,2,128]{3,2,1,0:T(2,128)S(1)} %get-tuple-element.58), channel_id=1, source_target_pairs={{0,4},{4,8},{8,12},{12,16},{16,20},{20,24},{24,28},{28,32},{32,36}... | collective-permute-start | bytes 98312 | tf_op jit(solution)/shard_map/ppermute | solution.py:20
  17.6 0.7 iota_compare_fusion.1
  18.3 4.3 %collective-permute-done.3 = f32[1,32,2,128]{3,2,1,0:T(2,128)S(1)} collective-permute-done((f32[1,32,2,128]{3,2,1,0:T(2,128)S(1)}, f32[1,32,2,128]{3,2,1,0:T(2,128)S(1)}, u32[]{:S(2)}, u32[]{:S(2)}) %collective-permute-start.3) | collective-permute-done | bytes 32800 | tf_op jit(solution)/shard_map/ppermute | solution.py:20
  22.6 1.0 multiply_convert_fusion.2
  23.6 0.5 convolution_convert_fusion.1
  24.1 2.1 %copy.22 = bf16[128,16,2,128]{3,2,1,0:T(2,128)(2,1)} copy(bf16[128,16,2,128]{3,0,2,1:T(8,128)(2,1)S(1)} %convolution_convert_fusion.1) | data formatting | bytes 2097152 | tf_op jit(solution)/shard_map/convert_element_type | solution.py:83
  26.2 19.1 %all-to-all-start = ((bf16[128,16,2,128]{3,2,1,0:T(2,128)(2,1)}), bf16[128,16,2,128]{3,2,1,0:T(2,128)(2,1)S(1)}, u32[]{:S(2)}, u32[]{:S(2)}) async-start(bf16[128,16,2,128]{3,2,1,0:T(2,128)(2,1)} %copy.22), calls=%async_computation | async-start | bytes 2097152 | tf_op jit(solution)/shard_map/all_to_all | solution.py:87
  46.6 0.7 constant_dynamic-slice_fusion.1
  47.7 53.0 %all-to-all-done = bf16[128,16,2,128]{3,2,1,0:T(2,128)(2,1)S(1)} async-done(((bf16[128,16,2,128]{3,2,1,0:T(2,128)(2,1)}), bf16[128,16,2,128]{3,2,1,0:T(2,128)(2,1)S(1)}, u32[]{:S(2)}, u32[]{:S(2)}) %all-to-all-start) | async-done | bytes 1048608 | tf_op jit(solution)/shard_map/all_to_all | solution.py:87
  100.7 9.9 %while.12 = (s32[]{:T(128)}, bf16[16,256,128]{2,1,0:T(8,128)(2,1)S(1)}, f32[16,256]{1,0:T(8,128)S(1)}, f32[256]{0:T(256)S(1)}, bf16[16,256,128]{2,1,0:T(8,128)(2...) while((s32[]{:T(128)}, bf16[16,256,128]{2,1,0:T(8,128)(2,1)S(1)}, f32[16,256]{1,0:T(8,128)S(1)}, ...), condition=%wide.region_2.3_spmd, body=%wide.region_0.2_spmd.sunk | while | flops 33914624 | bytes 791657 | solution.py:97
  100.7 0.2 fusion.63
  101.0 0.3 fusion.64
  101.3 0.2 fusion.63
  101.6 0.3 fusion.64
  102.0 0.2 fusion.63
  102.2 0.3 fusion.64
  102.6 0.2 fusion.63
  102.9 0.3 fusion.64
  103.2 0.2 fusion.63
  103.5 0.3 fusion.64
  103.8 0.2 fusion.63
  104.1 0.3 fusion.64
  104.5 0.2 fusion.63
  104.7 0.3 fusion.64
  105.1 0.2 fusion.63
  105.4 0.3 fusion.64
  105.7 0.2 fusion.63
  106.0 0.3 fusion.64
  106.3 0.2 fusion.63
  106.6 0.3 fusion.64
  107.0 0.2 fusion.63
  107.2 0.3 fusion.64
  107.6 0.2 fusion.63
  107.9 0.3 fusion.64
  108.2 0.2 fusion.63
  108.5 0.3 fusion.64
  108.8 0.2 fusion.63
  109.1 0.3 fusion.64
  109.4 0.2 fusion.63
  109.7 0.3 fusion.64
  110.1 0.2 fusion.63
  110.3 0.3 fusion.64
  110.7 0.2 copy.24
  110.9 61.9 %all_to_all.10 = bf16[128,16,2,128]{3,1,2,0:T(8,128)(2,1)S(1)} all-to-all(bf16[128,16,2,128]{3,1,2,0:T(8,128)(2,1)S(1)} %copy.24), channel_id=1, replica_groups=mesh['tile'=128,'lev'=4] {'tile'}, dimensions={0} | all-to-all | bytes 2097152 | tf_op jit(solution)/shard_map/all_to_all | solution.py:100
  172.7 0.8 fusion.8
  173.7 3.4 %collective-permute-start.4 = (f32[1,32,2,128]{3,2,1,0:T(2,128)S(1)}, f32[1,32,2,128]{3,2,1,0:T(2,128)S(1)}, u32[]{:S(2)}, u32[]{:S(2)}) collective-permute-start(f32[1,32,2,128]{3,2,1,0:T(2,128)S(1)} %get-tuple-element.55), channel_id=1, source_target_pairs={{4,0},{8,4},{12,8},{16,12},{20,16},{24,20},{28,24},{32,28},{36,32}... | collective-permute-start | bytes 98312 | tf_op jit(solution)/shard_map/ppermute | solution.py:22
  177.1 1.9 collective-permute-start.5
  179.1 5.4 %collective-permute-done.5 = f32[1,32,2,128]{3,2,1,0:T(2,128)S(1)} collective-permute-done((f32[1,32,2,128]{3,2,1,0:T(2,128)S(1)}, f32[1,32,2,128]{3,2,1,0:T(2,128)S(1)}, u32[]{:S(2)}, u32[]{:S(2)}) %collective-permute-start.5) | collective-permute-done | bytes 32800 | tf_op jit(solution)/shard_map/ppermute | solution.py:20
  184.5 0.1 multiply_add_fusion.1
  184.6 1.9 collective-permute-start.6
  186.6 2.4 %collective-permute-start.7 = (f32[1,32,2,128]{3,2,1,0:T(2,128)S(1)}, f32[1,32,2,128]{3,2,1,0:T(2,128)S(1)}, u32[]{:S(2)}, u32[]{:S(2)}) collective-permute-start(f32[1,32,2,128]{3,2,1,0:T(2,128)S(1)} %get-tuple-element.54), channel_id=1, source_target_pairs={{0,4},{4,8},{8,12},{12,16},{16,20},{20,24},{24,28},{28,32},{32,36}... | collective-permute-start | bytes 98312 | tf_op jit(solution)/shard_map/ppermute | solution.py:20
  189.0 0.6 reduce_sum.17
  189.6 2.6 %collective-permute-start.8 = (f32[1]{0:T(128)}, f32[1]{0:T(128)}, u32[]{:S(2)}, u32[]{:S(2)}) collective-permute-start(f32[1]{0:T(128)} %bitcast.17), channel_id=1, source_target_pairs={{0,1},{1,0},{2,3},{3,2},{4,5},{5,4},{6,7},{7,6},{8,9},{9,8},{10,11... | collective-permute-start | bytes 20 | tf_op jit(solution)/shard_map/ppermute | solution.py:104
  192.2 3.0 %collective-permute-done.8 = f32[1]{0:T(128)} collective-permute-done((f32[1]{0:T(128)}, f32[1]{0:T(128)}, u32[]{:S(2)}, u32[]{:S(2)}) %collective-permute-start.8) | collective-permute-done | bytes 36 | tf_op jit(solution)/shard_map/ppermute | solution.py:104
  196.5 4.4 %collective-permute-start.9 = (f32[1]{0:T(128)}, f32[1]{0:T(128)}, u32[]{:S(2)}, u32[]{:S(2)}) collective-permute-start(f32[1]{0:T(128)} %add.189), channel_id=1, source_target_pairs={{0,2},{1,3},{2,0},{3,1},{4,6},{5,7},{6,4},{7,5},{8,10},{9,11},{10,... | collective-permute-start | bytes 20 | tf_op jit(solution)/shard_map/ppermute | solution.py:104
  200.9 2.6 %collective-permute-done.9 = f32[1]{0:T(128)} collective-permute-done((f32[1]{0:T(128)}, f32[1]{0:T(128)}, u32[]{:S(2)}, u32[]{:S(2)}) %collective-permute-start.9) | collective-permute-done | bytes 36 | tf_op jit(solution)/shard_map/ppermute | solution.py:104
  204.1 0.8 multiply_add_fusion
  (55 shorter events, 2.5 us)
Async XLA Ops:
  0.6 44.8 %copy-start = (s32[128,256]{1,0:T(8,128)S(1)}, s32[128,256]{1,0:T(8,128)}, u32[]{:S(2)}) copy-start(s32[128,256]{1,0:T(8,128)} %param.16) | copy-start | bytes 393220
  0.6 23.0 %copy-start.3 = (s32[1,128,16]{1,2,0:T(8,128)S(1)}, s32[1,128,16]{1,2,0:T(8,128)}, u32[]{:S(2)}) copy-start(s32[1,128,16]{1,2,0:T(8,128)} %param.14) | copy-start | bytes 24580
  1.5 6.5 %collective-permute-start = (f32[1,32,2,128]{3,2,1,0:T(2,128)S(1)}, f32[1,32,2,128]{3,2,1,0:T(2,128)S(1)}, u32[]{:S(2)}, u32[]{:S(2)}) collective-permute-start(f32[1,32,2,128]{3,2,1,0:T(2,128)S(1)} %get-tuple-element.61), channel_id=1, source_target_pairs={{4,0},{8,4},{12,8},{16,12},{20,16},{24,20},{28,24},{32,28},{36,32}... | collective-permute-start | bytes 98312 | tf_op jit(solution)/shard_map/ppermute | solution.py:22
  5.1 7.3 %collective-permute-start.1 = (f32[1,32,2,128]{3,2,1,0:T(2,128)S(1)}, f32[1,32,2,128]{3,2,1,0:T(2,128)S(1)}, u32[]{:S(2)}, u32[]{:S(2)}) collective-permute-start(f32[1,32,2,128]{3,2,1,0:T(2,128)S(1)} %get-tuple-element.62), channel_id=1, source_target_pairs={{0,4},{4,8},{8,12},{12,16},{16,20},{20,24},{24,28},{28,32},{32,36}... | collective-permute-start | bytes 98312 | tf_op jit(solution)/shard_map/ppermute | solution.py:20
  13.3 5.0 %collective-permute-start.2 = (f32[1,32,2,128]{3,2,1,0:T(2,128)S(1)}, f32[1,32,2,128]{3,2,1,0:T(2,128)S(1)}, u32[]{:S(2)}, u32[]{:S(2)}) collective-permute-start(f32[1,32,2,128]{3,2,1,0:T(2,128)S(1)} %get-tuple-element.57), channel_id=1, source_target_pairs={{4,0},{8,4},{12,8},{16,12},{20,16},{24,20},{28,24},{32,28},{36,32}... | collective-permute-start | bytes 98312 | tf_op jit(solution)/shard_map/ppermute | solution.py:22
  15.2 7.3 %collective-permute-start.3 = (f32[1,32,2,128]{3,2,1,0:T(2,128)S(1)}, f32[1,32,2,128]{3,2,1,0:T(2,128)S(1)}, u32[]{:S(2)}, u32[]{:S(2)}) collective-permute-start(f32[1,32,2,128]{3,2,1,0:T(2,128)S(1)} %get-tuple-element.58), channel_id=1, source_target_pairs={{0,4},{4,8},{8,12},{12,16},{16,20},{20,24},{24,28},{28,32},{32,36}... | collective-permute-start | bytes 98312 | tf_op jit(solution)/shard_map/ppermute | solution.py:20
  26.2 19.1 %copy-start.2 = (bf16[1,256,32]{1,2,0:T(8,128)(2,1)S(1)}, bf16[1,256,32]{1,2,0:T(8,128)(2,1)}, u32[]{:S(2)}) copy-start(bf16[1,256,32]{1,2,0:T(8,128)(2,1)} %param.15) | copy-start | bytes 49156
  26.2 74.6 %all-to-all-start = ((bf16[128,16,2,128]{3,2,1,0:T(2,128)(2,1)}), bf16[128,16,2,128]{3,2,1,0:T(2,128)(2,1)S(1)}, u32[]{:S(2)}, u32[]{:S(2)}) async-start(bf16[128,16,2,128]{3,2,1,0:T(2,128)(2,1)} %copy.22), calls=%async_computation | async-start | bytes 2097152 | tf_op jit(solution)/shard_map/all_to_all | solution.py:87
  172.7 0.8 copy-start.1
  172.7 11.7 %copy-start.4 = (f32[128]{0:T(128)S(1)}, f32[128]{0:T(128)}, u32[]{:S(2)}) copy-start(f32[128]{0:T(128)} %param.12) | copy-start | bytes 1540
  173.7 5.3 %collective-permute-start.4 = (f32[1,32,2,128]{3,2,1,0:T(2,128)S(1)}, f32[1,32,2,128]{3,2,1,0:T(2,128)S(1)}, u32[]{:S(2)}, u32[]{:S(2)}) collective-permute-start(f32[1,32,2,128]{3,2,1,0:T(2,128)S(1)} %get-tuple-element.55), channel_id=1, source_target_pairs={{4,0},{8,4},{12,8},{16,12},{20,16},{24,20},{28,24},{32,28},{36,32}... | collective-permute-start | bytes 98312 | tf_op jit(solution)/shard_map/ppermute | solution.py:22
  177.1 7.3 %collective-permute-start.5 = (f32[1,32,2,128]{3,2,1,0:T(2,128)S(1)}, f32[1,32,2,128]{3,2,1,0:T(2,128)S(1)}, u32[]{:S(2)}, u32[]{:S(2)}) collective-permute-start(f32[1,32,2,128]{3,2,1,0:T(2,128)S(1)} %get-tuple-element.56), channel_id=1, source_target_pairs={{0,4},{4,8},{8,12},{12,16},{16,20},{20,24},{24,28},{28,32},{32,36}... | collective-permute-start | bytes 98312 | tf_op jit(solution)/shard_map/ppermute | solution.py:20
  184.6 19.4 %collective-permute-start.6 = (f32[1,32,2,128]{3,2,1,0:T(2,128)S(1)}, f32[1,32,2,128]{3,2,1,0:T(2,128)S(1)}, u32[]{:S(2)}, u32[]{:S(2)}) collective-permute-start(f32[1,32,2,128]{3,2,1,0:T(2,128)S(1)} %get-tuple-element.53), channel_id=1, source_target_pairs={{4,0},{8,4},{12,8},{16,12},{20,16},{24,20},{28,24},{32,28},{36,32}... | collective-permute-start | bytes 98312 | tf_op jit(solution)/shard_map/ppermute | solution.py:22
  186.6 17.5 %collective-permute-start.7 = (f32[1,32,2,128]{3,2,1,0:T(2,128)S(1)}, f32[1,32,2,128]{3,2,1,0:T(2,128)S(1)}, u32[]{:S(2)}, u32[]{:S(2)}) collective-permute-start(f32[1,32,2,128]{3,2,1,0:T(2,128)S(1)} %get-tuple-element.54), channel_id=1, source_target_pairs={{0,4},{4,8},{8,12},{12,16},{16,20},{20,24},{24,28},{28,32},{32,36}... | collective-permute-start | bytes 98312 | tf_op jit(solution)/shard_map/ppermute | solution.py:20
  189.6 5.7 %collective-permute-start.8 = (f32[1]{0:T(128)}, f32[1]{0:T(128)}, u32[]{:S(2)}, u32[]{:S(2)}) collective-permute-start(f32[1]{0:T(128)} %bitcast.17), channel_id=1, source_target_pairs={{0,1},{1,0},{2,3},{3,2},{4,5},{5,4},{6,7},{7,6},{8,9},{9,8},{10,11... | collective-permute-start | bytes 20 | tf_op jit(solution)/shard_map/ppermute | solution.py:104
  196.5 7.0 %collective-permute-start.9 = (f32[1]{0:T(128)}, f32[1]{0:T(128)}, u32[]{:S(2)}, u32[]{:S(2)}) collective-permute-start(f32[1]{0:T(128)} %add.189), channel_id=1, source_target_pairs={{0,2},{1,3},{2,0},{3,1},{4,6},{5,7},{6,4},{7,5},{8,10},{9,11},{10,... | collective-permute-start | bytes 20 | tf_op jit(solution)/shard_map/ppermute | solution.py:104
